TPU v7x, 32 devices: a whole 2x2x4 slice. The times are simulated.
32 devices in a mesh: ctx: 8 (over z, y), shard: 4 (over x, core).
Axes of the slice: x: 2, y: 2, z: 4, core: 2. Of those that a mesh axis runs over, the one named last changes fastest.
Arguments:
- block_in: bfloat16 [1024, 1024], P('ctx'), may hold values from -6 to 6
- attn_gain: float32 [1024], replicated, may hold values from 0.5 to 1.5
- q_weight: bfloat16 [1024, 1024], P(None, 'shard'), may hold values from -0.1875 to 0.1875
- k_weight: bfloat16 [1024, 512], P(None, 'shard'), may hold values from -0.1875 to 0.1875
- v_weight: bfloat16 [1024, 512], P(None, 'shard'), may hold values from -0.1875 to 0.1875
- o_weight: bfloat16 [1024, 1024], P('shard'), may hold values from -1.5 to 1.5
- moe_gain: float32 [1024], replicated, may hold values from 0.5 to 1.5
- router_weight: bfloat16 [1024, 16], replicated, may hold values from -0.1875 to 0.1875
- expert_gate: bfloat16 [16, 1024, 512], P('shard'), may hold values from -0.1875 to 0.1875
- expert_up: bfloat16 [16, 1024, 512], P('shard'), may hold values from -0.1875 to 0.1875
- expert_down: bfloat16 [16, 512, 1024], P('shard'), may hold values from -0.5 to 0.5
- routes: int32 [1024, 8], P('ctx'), may hold values from 0 to 15, all different within a row; in each aligned block of 128 rows (0 to 127, 128 to 255, ...) at most 112 rows name the same one
- out_grad: float32 [1024, 1024], P('ctx'), may hold values from -6 to 6
Outputs:
- block_out: float32 [1024, 1024], P('ctx')
- in_grad: float32 [1024, 1024], P('ctx')
- attn_gain_grad: float32 [1024], P('ctx')
- q_weight_grad: float32 [1024, 1024], P('ctx', 'shard')
- k_weight_grad: float32 [1024, 512], P('ctx', 'shard')
- v_weight_grad: float32 [1024, 512], P('ctx', 'shard')
- o_weight_grad: float32 [1024, 1024], P('shard', 'ctx')
- moe_gain_grad: float32 [1024], P('ctx')
- router_grad: float32 [1024, 16], P('ctx')
- gate_grad: float32 [16, 1024, 512], P('shard', 'ctx')
- up_grad: float32 [16, 1024, 512], P('shard', 'ctx')
- down_grad: float32 [16, 512, 1024], P('shard', None, 'ctx')
Inputs may be any that keep to these rules, and one draw needn't show every extreme that they name: `routes`: each row names 8 different experts; in each aligned block of 128 rows (128; a device may hold several) no expert is named by more than 112 rows.
All inputs are finite; a program needn't handle non-finite values.
Results may differ from a plain program's by a relative error of at most 0.015.
Values may be sent and summed in bfloat16 or wider, within the bound.
No kernel may reach another device: no remote copies, remote signals or barrier semaphores. Data moves between devices by JAX's collectives and lax.ppermute only.
A program may use at most 128 MiB of HBM per device.

v0:
```python
import math
import jax
import jax.numpy as jnp
from jax import lax
from jax.sharding import PartitionSpec as P

HD = 64
CAP = 112
NORM_EPS = 1e-06
ROPE_BASE = 10000.0


def rope_tables(positions, head_width):
    half_width = head_width // 2
    freq_steps = jnp.arange(half_width, dtype=jnp.float32) * (2.0 / head_width)
    inv_freq = jnp.exp(-math.log(ROPE_BASE) * freq_steps)
    angles = positions.astype(jnp.float32)[:, None] * inv_freq[None, :]
    cos_tab = jnp.concatenate([jnp.cos(angles), jnp.cos(angles)], axis=1)
    sin_tab = jnp.concatenate([jnp.sin(angles), jnp.sin(angles)], axis=1)
    return (cos_tab, sin_tab)


def rotate_heads(head_vals, cos_tab, sin_tab):
    half_width = head_vals.shape[-1] // 2
    turned = jnp.concatenate([-head_vals[..., half_width:], head_vals[..., :half_width]], axis=-1)
    return head_vals * cos_tab[:, None, :] + turned * sin_tab[:, None, :]


def unrotate_heads(head_grads, cos_tab, sin_tab):
    half_width = head_grads.shape[-1] // 2
    scaled = head_grads * sin_tab[:, None, :]
    back = jnp.concatenate([scaled[..., half_width:], -scaled[..., :half_width]], axis=-1)
    return head_grads * cos_tab[:, None, :] + back


def rms_forward(inputs, gain):
    inverse = lax.rsqrt(jnp.mean(inputs * inputs, axis=-1, keepdims=True) + NORM_EPS)
    return (inputs * inverse * gain, inverse)


def rms_backward(inputs, inverse, gain, grads):
    scaled = grads * gain
    inner = jnp.mean(scaled * inputs, axis=-1, keepdims=True)
    d_inputs = inverse * scaled - inputs * inverse * inverse * inverse * inner
    d_gain = jnp.sum(grads * inputs * inverse, axis=0)
    return (d_inputs, d_gain)


def slot_tables(routes, n_experts):
    expert_ids = jnp.arange(n_experts, dtype=jnp.int32)
    expert_hits = jnp.sum(
        (routes[:, :, None] == expert_ids[None, None, :]).astype(jnp.int32), axis=1
    )
    earlier_hits = jnp.cumsum(expert_hits, axis=0) - expert_hits
    slot_ids = jnp.take_along_axis(earlier_hits, routes, axis=1)
    return (expert_hits, earlier_hits, slot_ids)


def spread_to_experts(values_tk, routes, n_experts):
    expert_ids = jnp.arange(n_experts, dtype=jnp.int32)
    return jnp.sum(
        jnp.where(routes[:, :, None] == expert_ids[None, None, :], values_tk[:, :, None], 0.0),
        axis=1,
    )


def slot_rows(expert_hits, earlier_hits, weight_table, first_expert, expert_count, capacity):
    local_hits = lax.dynamic_slice_in_dim(expert_hits, first_expert, expert_count, 1).T
    local_earlier = lax.dynamic_slice_in_dim(earlier_hits, first_expert, expert_count, 1).T
    local_weight = lax.dynamic_slice_in_dim(weight_table, first_expert, expert_count, 1).T
    slot_range = jnp.arange(capacity, dtype=jnp.int32)
    matched = (local_hits[:, None, :] > 0) & (
        local_earlier[:, None, :] == slot_range[None, :, None]
    )
    row_range = jnp.arange(expert_hits.shape[0], dtype=jnp.int32)
    row_ids = jnp.sum(jnp.where(matched, row_range[None, None, :], 0), axis=2)
    row_valid = jnp.any(matched, axis=2)
    slot_weight = jnp.sum(jnp.where(matched, local_weight[:, None, :], 0.0), axis=2)
    return (row_ids, row_valid, slot_weight)


def body(
    block_in,
    attn_gain,
    q_weight,
    k_weight,
    v_weight,
    o_weight,
    moe_gain,
    router_weight,
    expert_gate,
    expert_up,
    expert_down,
    routes,
    out_grad,
):
    row_count = block_in.shape[0]
    model_width = block_in.shape[1]
    seq_len = row_count * lax.axis_size("ctx")
    q_local = q_weight.shape[1] // HD
    kv_local = k_weight.shape[1] // HD
    group = q_local // kv_local
    scale = HD ** (-0.5)
    key_block = math.gcd(512, seq_len)
    first_row = lax.axis_index("ctx") * row_count
    blocks_needed = (first_row + row_count + key_block - 1) // key_block
    positions = first_row + jnp.arange(row_count, dtype=jnp.int32)
    cos_tab, sin_tab = rope_tables(positions, HD)
    resid_in = block_in.astype(jnp.float32)
    normed_one, inverse_one = rms_forward(resid_in, attn_gain)
    normed_one = normed_one.astype(jnp.bfloat16)
    query_rot = rotate_heads(
        jnp.dot(normed_one, q_weight, preferred_element_type=jnp.float32).reshape(
            row_count, q_local, HD
        ),
        cos_tab,
        sin_tab,
    ).astype(jnp.bfloat16)
    query_groups = query_rot.reshape(row_count, kv_local, group, HD)
    key_rot = (
        rotate_heads(
            jnp.dot(normed_one, k_weight, preferred_element_type=jnp.float32).reshape(
                row_count, kv_local, HD
            ),
            cos_tab,
            sin_tab,
        )
        .astype(jnp.bfloat16)
        .reshape(row_count, kv_local * HD)
    )
    value_proj = jnp.dot(normed_one, v_weight, preferred_element_type=jnp.float32).astype(
        jnp.bfloat16
    )

    def masked_scores(key_piece, key_start):
        piece_len = key_piece.shape[0]
        raw = (
            jnp.einsum(
                "tngd,jnd->ngtj",
                query_groups,
                key_piece.reshape(piece_len, kv_local, HD),
                preferred_element_type=jnp.float32,
            )
            * scale
        )
        key_pos = key_start + jnp.arange(piece_len, dtype=jnp.int32)
        allowed = key_pos[None, :] <= positions[:, None]
        return jnp.where(allowed[None, None], raw, -jnp.inf)

    running_top = jnp.full((kv_local, group, row_count), -1e30, jnp.float32)
    scores = masked_scores(lax.all_gather(key_rot, "ctx", axis=0, tiled=True), jnp.int32(0))
    new_top = jnp.maximum(running_top, jnp.max(scores, axis=-1))
    new_total = jnp.sum(jnp.exp(scores - new_top[..., None]), axis=-1)
    log_total = new_top + jnp.log(new_total)
    key_piece = lax.all_gather(key_rot, "ctx", axis=0, tiled=True)
    value_piece = lax.all_gather(value_proj, "ctx", axis=0, tiled=True)
    scores = masked_scores(key_piece, jnp.int32(0))
    probs = jnp.exp(scores - log_total[..., None]).astype(jnp.bfloat16)
    piece_len = value_piece.shape[0]
    running_acc = jnp.einsum(
        "ngtj,jnd->ngtd",
        probs,
        value_piece.reshape(piece_len, kv_local, HD),
        preferred_element_type=jnp.float32,
    )
    heads_out = (
        running_acc.transpose(2, 0, 1, 3).reshape(row_count, q_local * HD).astype(jnp.bfloat16)
    )
    resid_mid = resid_in + lax.psum(
        jnp.dot(heads_out, o_weight, preferred_element_type=jnp.float32), "shard"
    )
    normed_two, inverse_two = rms_forward(resid_mid, moe_gain)
    normed_two = normed_two.astype(jnp.bfloat16)
    logits = jnp.dot(normed_two, router_weight, preferred_element_type=jnp.float32)
    gate = jax.nn.softmax(jnp.take_along_axis(logits, routes, axis=1), axis=-1)
    local_count = expert_gate.shape[0]
    n_experts = local_count * lax.axis_size("shard")
    first_expert = lax.axis_index("shard") * local_count
    expert_hits, earlier_hits, slot_ids = slot_tables(routes, n_experts)
    gate_table = spread_to_experts(gate, routes, n_experts)
    row_ids, row_valid, slot_weight = slot_rows(
        expert_hits, earlier_hits, gate_table, first_expert, local_count, CAP
    )
    buffer = jnp.where(row_valid[..., None], normed_two[row_ids], jnp.zeros((), jnp.bfloat16))
    pre_gate = jnp.einsum("ecd,edf->ecf", buffer, expert_gate, preferred_element_type=jnp.float32)
    pre_up = jnp.einsum("ecd,edf->ecf", buffer, expert_up, preferred_element_type=jnp.float32)
    sig_gate = jax.nn.sigmoid(pre_gate)
    hidden = (pre_gate * sig_gate * pre_up).astype(jnp.bfloat16)
    expert_out = jnp.einsum("ecf,efd->ecd", hidden, expert_down, preferred_element_type=jnp.float32)
    is_local = (routes >= first_expert) & (routes < first_expert + local_count)
    flat_ids = jnp.where(is_local, (routes - first_expert) * CAP + slot_ids, 0)
    picked = expert_out.reshape(local_count * CAP, model_width)[flat_ids]
    moe_part = jnp.sum(jnp.where(is_local, gate, 0.0)[..., None] * picked, axis=1)
    d_gate_part = jnp.where(is_local, jnp.sum(picked * out_grad[:, None, :], axis=-1), 0.0)
    block_out = resid_mid + lax.psum(moe_part.astype(jnp.bfloat16), "shard").astype(jnp.float32)
    d_expert_out = (jnp.where(row_valid, slot_weight, 0.0)[..., None] * out_grad[row_ids]).astype(
        jnp.bfloat16
    )
    d_hidden = jnp.einsum(
        "ecd,efd->ecf", d_expert_out, expert_down, preferred_element_type=jnp.float32
    )
    down_part = jnp.einsum("ecf,ecd->efd", hidden, d_expert_out, preferred_element_type=jnp.float32)
    d_silu = sig_gate * (1.0 + pre_gate * (1.0 - sig_gate))
    d_pre_gate = (d_hidden * pre_up * d_silu).astype(jnp.bfloat16)
    d_pre_up = (d_hidden * pre_gate * sig_gate).astype(jnp.bfloat16)
    gate_part = jnp.einsum("ecd,ecf->edf", buffer, d_pre_gate, preferred_element_type=jnp.float32)
    up_part = jnp.einsum("ecd,ecf->edf", buffer, d_pre_up, preferred_element_type=jnp.float32)
    d_buffer = jnp.einsum(
        "ecf,edf->ecd", d_pre_gate, expert_gate, preferred_element_type=jnp.float32
    ) + jnp.einsum("ecf,edf->ecd", d_pre_up, expert_up, preferred_element_type=jnp.float32)
    d_normed_part = jnp.sum(
        jnp.where(
            is_local[..., None], d_buffer.reshape(local_count * CAP, model_width)[flat_ids], 0.0
        ),
        axis=1,
    )
    d_normed_exp, d_gate = lax.psum((d_normed_part, d_gate_part), "shard")
    d_chosen = gate * (d_gate - jnp.sum(gate * d_gate, axis=-1, keepdims=True))
    d_logits = spread_to_experts(d_chosen, routes, n_experts)
    router_f = router_weight.astype(jnp.float32)
    d_normed_two = d_normed_exp + jnp.dot(d_logits, router_f.T, precision=lax.Precision.HIGHEST)
    router_part = jnp.dot(
        normed_two.astype(jnp.float32).T, d_logits, precision=lax.Precision.HIGHEST
    )
    d_resid_norm, moe_gain_part = rms_backward(resid_mid, inverse_two, moe_gain, d_normed_two)
    d_resid_mid = out_grad + d_resid_norm
    d_mid_b = d_resid_mid.astype(jnp.bfloat16)
    o_part = jnp.dot(heads_out.T, d_mid_b, preferred_element_type=jnp.float32)
    d_heads = jnp.dot(d_mid_b, o_weight.T, preferred_element_type=jnp.float32).astype(jnp.bfloat16)
    d_head_groups = d_heads.reshape(row_count, kv_local, group, HD)
    delta = jnp.sum(
        d_heads.astype(jnp.float32).reshape(row_count, kv_local, group, HD)
        * heads_out.astype(jnp.float32).reshape(row_count, kv_local, group, HD),
        axis=-1,
    ).transpose(1, 2, 0)
    keys_back, values_back = (
        lax.all_gather(key_rot, "ctx", axis=0, tiled=True),
        lax.all_gather(value_proj, "ctx", axis=0, tiled=True),
    )

    def key_step(block_idx, carry):
        d_query_acc, d_key_term, d_value_term = carry
        key_start = block_idx * key_block
        key_piece = lax.dynamic_slice_in_dim(keys_back, key_start, key_block, 0)
        value_piece = lax.dynamic_slice_in_dim(values_back, key_start, key_block, 0)
        scores = masked_scores(key_piece, key_start)
        probs = jnp.exp(scores - log_total[..., None])
        key_heads = key_piece.reshape(key_block, kv_local, HD)
        value_heads = value_piece.reshape(key_block, kv_local, HD)
        d_probs = jnp.einsum(
            "tngd,jnd->ngtj", d_head_groups, value_heads, preferred_element_type=jnp.float32
        )
        d_scores = (probs * (d_probs - delta[..., None])).astype(jnp.bfloat16)
        d_query_acc = d_query_acc + scale * jnp.einsum(
            "ngtj,jnd->tngd", d_scores, key_heads, preferred_element_type=jnp.float32
        )
        d_key_blk = scale * jnp.einsum(
            "ngtj,tngd->jnd", d_scores, query_groups, preferred_element_type=jnp.float32
        )
        d_value_blk = jnp.einsum(
            "ngtj,tngd->jnd",
            probs.astype(jnp.bfloat16),
            d_head_groups,
            preferred_element_type=jnp.float32,
        )
        d_key_term = lax.dynamic_update_slice_in_dim(
            d_key_term, d_key_blk.reshape(key_block, kv_local * HD), key_start, 0
        )
        d_value_term = lax.dynamic_update_slice_in_dim(
            d_value_term, d_value_blk.reshape(key_block, kv_local * HD), key_start, 0
        )
        return (d_query_acc, d_key_term, d_value_term)

    zero_terms = jnp.zeros((seq_len, kv_local * HD), jnp.float32)
    d_query_acc, d_key_term, d_value_term = lax.fori_loop(
        0,
        blocks_needed,
        key_step,
        (jnp.zeros((row_count, kv_local, group, HD), jnp.float32), zero_terms, zero_terms),
    )
    d_key_own, d_value_own = (
        lax.psum_scatter(d_key_term, "ctx", scatter_dimension=0, tiled=True),
        lax.psum_scatter(d_value_term, "ctx", scatter_dimension=0, tiled=True),
    )
    d_query = (
        unrotate_heads(d_query_acc.reshape(row_count, q_local, HD), cos_tab, sin_tab)
        .astype(jnp.bfloat16)
        .reshape(row_count, q_local * HD)
    )
    d_key = (
        unrotate_heads(d_key_own.reshape(row_count, kv_local, HD), cos_tab, sin_tab)
        .astype(jnp.bfloat16)
        .reshape(row_count, kv_local * HD)
    )
    d_value = d_value_own.astype(jnp.bfloat16)
    q_part = jnp.dot(normed_one.T, d_query, preferred_element_type=jnp.float32)
    k_part = jnp.dot(normed_one.T, d_key, preferred_element_type=jnp.float32)
    v_part = jnp.dot(normed_one.T, d_value, preferred_element_type=jnp.float32)
    d_normed_part_one = (
        jnp.dot(d_query, q_weight.T, preferred_element_type=jnp.float32)
        + jnp.dot(d_key, k_weight.T, preferred_element_type=jnp.float32)
        + jnp.dot(d_value, v_weight.T, preferred_element_type=jnp.float32)
    )
    d_normed_one = lax.psum(d_normed_part_one, "shard")
    d_resid_first, attn_gain_part = rms_backward(resid_in, inverse_one, attn_gain, d_normed_one)
    in_grad = d_resid_mid + d_resid_first
    (
        attn_gain_grad,
        q_weight_grad,
        k_weight_grad,
        v_weight_grad,
        o_weight_grad,
        moe_gain_grad,
        router_grad,
        gate_grad,
        up_grad,
        down_grad,
    ) = (
        lax.psum_scatter(attn_gain_part, "ctx", scatter_dimension=0, tiled=True),
        lax.psum_scatter(q_part, "ctx", scatter_dimension=0, tiled=True),
        lax.psum_scatter(k_part, "ctx", scatter_dimension=0, tiled=True),
        lax.psum_scatter(v_part, "ctx", scatter_dimension=0, tiled=True),
        lax.psum_scatter(o_part, "ctx", scatter_dimension=1, tiled=True),
        lax.psum_scatter(moe_gain_part, "ctx", scatter_dimension=0, tiled=True),
        lax.psum_scatter(router_part, "ctx", scatter_dimension=0, tiled=True),
        lax.psum_scatter(gate_part, "ctx", scatter_dimension=1, tiled=True),
        lax.psum_scatter(up_part, "ctx", scatter_dimension=1, tiled=True),
        lax.psum_scatter(down_part, "ctx", scatter_dimension=2, tiled=True),
    )
    return (
        block_out,
        in_grad,
        attn_gain_grad,
        q_weight_grad,
        k_weight_grad,
        v_weight_grad,
        o_weight_grad,
        moe_gain_grad,
        router_grad,
        gate_grad,
        up_grad,
        down_grad,
    )


def solution(mesh):
    in_specs = (
        P("ctx", None),
        P(),
        P(None, "shard"),
        P(None, "shard"),
        P(None, "shard"),
        P("shard", None),
        P(),
        P(),
        P("shard", None, None),
        P("shard", None, None),
        P("shard", None, None),
        P("ctx", None),
        P("ctx", None),
    )
    out_specs = (
        P("ctx", None),
        P("ctx", None),
        P("ctx"),
        P("ctx", "shard"),
        P("ctx", "shard"),
        P("ctx", "shard"),
        P("shard", "ctx"),
        P("ctx"),
        P("ctx", None),
        P("shard", "ctx", None),
        P("shard", "ctx", None),
        P("shard", None, "ctx"),
    )
    return jax.shard_map(body, mesh=mesh, in_specs=in_specs, out_specs=out_specs, check_vma=False)
```

profile of v0, /device:TPU:0, one launch (start us, length us, event | category | flops | bytes accessed | tf_op | source)
XLA Modules:
  0.0 1194.1 jit_solution(7015718147966698272)
XLA Ops:
  7.3 1.1 fusion.29
  8.4 1.3 convolution_convert_fusion.2
  9.8 1.4 fusion.71
  11.3 1.5 fusion.69
  13.0 28.3 %all_gather.4 = bf16[1024,128]{0,1:T(8,128)(2,1)S(1)} all-gather(bf16[128,128]{0,1:T(8,128)(2,1)S(1)} %fusion.48), channel_id=1, replica_groups=mesh['ctx'=8,'shard'=4] {'ctx'}, dimensions={0}, use_global_device_ids=true | all-gather | bytes 294912 | tf_op jit(solution)/shard_map/all_gather | solution.py:155
  41.3 30.8 %all_gather.10 = bf16[1024,128]{1,0:T(8,128)(2,1)S(1)} all-gather(bf16[128,128]{1,0:T(8,128)(2,1)S(1)} %convolution_convert_fusion.2), channel_id=1, replica_groups=mesh['ctx'=8,'shard'=4] {'ctx'}, dimensions={0}, use_global_device_ids=true | all-gather | bytes 294912 | tf_op jit(solution)/shard_map/all_gather | solution.py:156
  73.7 1.1 fusion.77
  75.7 7.1 gather_fusion.5
  83.1 2.6 gather_fusion.2
  85.8 21.8 %all-reduce.8.cloned.1.call-done = f32[128,1024]{1,0:T(8,128)} async-done(((f32[128,1024]{1,0:T(8,128)}), f32[128,1024]{1,0:T(8,128)}) %all-reduce.8.cloned.1.call-update) | async-done | bytes 524304 | tf_op jit(solution)/shard_map/psum | solution.py:169
  107.6 1.2 multiply_reduce_fusion.2
  109.7 2.1 gather_fusion
  112.0 7.0 gather_fusion.4
  121.0 3.1 fusion.23
  124.4 1.8 multiply_convert_fusion.3
  126.2 1.2 copy-done.6
  128.1 5.4 gather_fusion.1
  133.6 4.6 fusion.15
  138.2 0.9 copy.150
  139.1 1.3 broadcast_select_fusion.5
  140.4 5.9 psum.38
  147.0 0.8 select_reduce_fusion
  148.4 4.5 multiply_convert_fusion.1
  153.0 1.4 fusion.80
  154.4 1.1 copy-done.15
  155.5 1.5 convolution_add_fusion
  157.0 5.4 gather_fusion.3
  162.4 4.4 fusion.14
  167.6 32.7 %all-reduce.12.cloned.1.call-done = f32[128,1024]{1,0:T(8,128)} async-done(((f32[128,1024]{1,0:T(8,128)}), f32[128,1024]{1,0:T(8,128)}) %all-reduce.12.cloned.1.call-update) | async-done | bytes 524304 | tf_op jit(solution)/shard_map/psum | solution.py:217
  200.3 2.9 multiply_reduce_fusion
  203.2 31.4 %all-reduce.10.cloned.1.call-done = bf16[128,1024]{1,0:T(8,128)(2,1)} async-done(((bf16[128,1024]{1,0:T(8,128)(2,1)}), bf16[128,1024]{1,0:T(8,128)(2,1)}) %all-reduce.10.cloned.1.call-update) | async-done | bytes 262160 | tf_op jit(solution)/shard_map/psum | solution.py:195
  234.6 2.1 subtract_add_fusion
  237.2 0.8 broadcast_in_dim.200.clone
  238.1 0.8 broadcast_in_dim.200
  239.0 2.9 while.15
  240.9 0.8 copy-done.20
  242.8 64.4 %reduce-scatter.11.cloned.1.call-done = f32[128,128]{0,1:T(8,128)} async-done(((f32[1024,128]{0,1:T(8,128)}), f32[128,128]{0,1:T(8,128)}) %reduce-scatter.11.cloned.1.call-update) | async-done | bytes 65552 | tf_op jit(solution)/shard_map/reduce_scatter | solution.py:282
  307.3 0.8 broadcast_multiply_fusion
  308.1 0.9 fusion.50
  309.0 1.2 convolution_add_fusion.2
  310.2 62.2 %reduce-scatter.13.cloned.1.call-done = f32[128,128]{0,1:T(8,128)} async-done(((f32[1024,128]{0,1:T(8,128)}), f32[128,128]{0,1:T(8,128)}) %reduce-scatter.13.cloned.1.call-update) | async-done | bytes 65552 | tf_op jit(solution)/shard_map/reduce_scatter | solution.py:283
  372.5 2.0 convolution_add_fusion.1
  374.5 0.8 fusion.82
  375.4 1.3 fusion.44
  376.9 1.1 fusion.51
  378.0 1.1 fusion.64
  379.3 1.3 fusion.66
  380.7 6.0 fusion.37
  386.8 1.1 copy-done.4
  388.0 4.6 fusion.20
  392.7 0.9 copy-done.25
  393.7 4.6 fusion.21
  400.1 7.4 all-reduce.14.cloned.1.call-done
  407.5 1.2 fusion.32
  408.7 21.6 %all-reduce.2 = (f32[1024]{0:T(1024)S(1)}, f32[1024]{0:T(1024)S(1)}) all-reduce(f32[1024]{0:T(1024)S(1)} %get-tuple-element.184, f32[1024]{0:T(1024)S(1)} %copy-done.46), channel_id=4, replica_groups=mesh['ctx'=8,'shard'=4] {'ctx'}, use_global_device_ids=true, to_apply=%region_30.31.clone | all-reduce | flops 2048 | bytes 16384
  431.6 2.0 fusion.28
  433.6 31.6 %reduce-scatter.23.cloned.1.call-done = f32[128,16]{0,1:T(8,128)} async-done(((f32[1024,16]{0,1:T(8,128)}), f32[128,16]{0,1:T(8,128)}) %reduce-scatter.23.cloned.1.call-update) | async-done | bytes 8208 | tf_op jit(solution)/shard_map/reduce_scatter | solution.py:325
  465.3 67.3 %reduce-scatter.21.cloned.1.call-done = f32[256,128]{1,0:T(8,128)} async-done(((f32[256,1024]{1,0:T(8,128)}), f32[256,128]{1,0:T(8,128)}) %reduce-scatter.21.cloned.1.call-update) | async-done | bytes 131088 | tf_op jit(solution)/shard_map/reduce_scatter | solution.py:323
  532.6 64.9 %reduce-scatter.19.cloned.1.call-done = f32[128,128]{1,0:T(8,128)} async-done(((f32[1024,128]{1,0:T(8,128)}), f32[128,128]{1,0:T(8,128)}) %reduce-scatter.19.cloned.1.call-update) | async-done | bytes 65552 | tf_op jit(solution)/shard_map/reduce_scatter | solution.py:322
  597.4 65.0 %reduce-scatter.17.cloned.1.call-done = f32[128,128]{1,0:T(8,128)} async-done(((f32[1024,128]{1,0:T(8,128)}), f32[128,128]{1,0:T(8,128)}) %reduce-scatter.17.cloned.1.call-update) | async-done | bytes 65552 | tf_op jit(solution)/shard_map/reduce_scatter | solution.py:321
  662.5 66.5 %reduce-scatter.15.cloned.1.call-done = f32[128,256]{1,0:T(8,128)} async-done(((f32[1024,256]{1,0:T(8,128)}), f32[128,256]{1,0:T(8,128)}) %reduce-scatter.15.cloned.1.call-update) | async-done | bytes 131088 | tf_op jit(solution)/shard_map/reduce_scatter | solution.py:320
  728.9 153.0 %reduce-scatter.29.cloned.1.call-done = f32[4,512,128]{2,1,0:T(8,128)} async-done(((f32[4,512,1024]{2,1,0:T(8,128)}), f32[4,512,128]{2,1,0:T(8,128)}) %reduce-scatter.29.cloned.1.call-update) | async-done | bytes 1048592 | tf_op jit(solution)/shard_map/reduce_scatter | solution.py:328
  881.9 152.7 %reduce-scatter.27.cloned.1.call-done = f32[4,128,512]{2,1,0:T(8,128)} async-done(((f32[4,1024,512]{2,1,0:T(8,128)}), f32[4,128,512]{2,1,0:T(8,128)}) %reduce-scatter.27.cloned.1.call-update) | async-done | bytes 1048592 | tf_op jit(solution)/shard_map/reduce_scatter | solution.py:327
  1034.6 153.0 %reduce-scatter.25.cloned.1.call-done = f32[4,128,512]{2,1,0:T(8,128)} async-done(((f32[4,1024,512]{2,1,0:T(8,128)}), f32[4,128,512]{2,1,0:T(8,128)}) %reduce-scatter.25.cloned.1.call-update) | async-done | bytes 1048592 | tf_op jit(solution)/shard_map/reduce_scatter | solution.py:326
  (217 shorter events, 15.6 us)
Async XLA Ops:
  7.2 66.5 %copy-start = (bf16[256,1024]{1,0:T(8,128)(2,1)S(1)}, bf16[256,1024]{1,0:T(8,128)(2,1)}, u32[]{:S(2)}) copy-start(bf16[256,1024]{1,0:T(8,128)(2,1)} %param.20) | copy-start | bytes 1572868
  7.2 100.4 %all-reduce.8.cloned.1.call-start = ((), (), s32[]{:S(2)}) async-start(), calls=%async_computation.10 | async-start | bytes 1048576 | tf_op jit(solution)/shard_map/psum | solution.py:169
  8.4 4.4 copy-start.44
  13.0 60.7 %copy-start.28 = (f32[128,64]{0,1:T(8,128)}, f32[128,64]{0,1:T(8,128)S(1)}, u32[]{:S(2)}) copy-start(f32[128,64]{0,1:T(8,128)S(1)} %get-tuple-element.243) | copy-start | bytes 98308
  13.0 60.7 %copy-start.30 = (f32[128,64]{0,1:T(8,128)}, f32[128,64]{0,1:T(8,128)S(1)}, u32[]{:S(2)}) copy-start(f32[128,64]{0,1:T(8,128)S(1)} %get-tuple-element.242) | copy-start | bytes 98308
  41.3 33.4 %copy-start.10 = (bf16[1024,128]{0,1:T(8,128)(2,1)}, bf16[1024,128]{0,1:T(8,128)(2,1)S(1)}, u32[]{:S(2)}) copy-start(bf16[1024,128]{0,1:T(8,128)(2,1)S(1)} %all_gather.4) | copy-start | bytes 786436
  72.3 2.4 copy-start.12
  72.3 2.5 copy-start.35
  73.2 2.4 copy-start.51
  74.8 125.5 %all-reduce.12.cloned.1.call-start = ((), (), s32[]{:S(2)}) async-start(), calls=%async_computation.12 | async-start | bytes 1048576 | tf_op jit(solution)/shard_map/psum | solution.py:217
  75.0 10.7 copy-start.50
  75.3 10.3 copy-start.43
  75.7 7.3 copy-start.1
  83.0 24.5 %copy-start.5 = (bf16[128,1024]{1,0:T(8,128)(2,1)S(1)}, bf16[128,1024]{1,0:T(8,128)(2,1)}, u32[]{:S(2)}) copy-start(bf16[128,1024]{1,0:T(8,128)(2,1)} %param.15) | copy-start | bytes 786436
  83.1 26.5 %copy-start.39 = (f32[1024]{0:T(1024)S(1)}, f32[1024]{0:T(1024)}, u32[]{:S(2)}) copy-start(f32[1024]{0:T(1024)} %param.21) | copy-start | bytes 12292
  85.8 38.3 %copy-start.41 = (pred[4,112]{1,0:T(4,128)(4,1)}, pred[4,112]{1,0:T(4,128)(4,1)S(1)}, u32[]{:S(2)}) copy-start(pred[4,112]{1,0:T(4,128)(4,1)S(1)} %fusion.40) | copy-start | bytes 1348
  108.8 3.0 copy-start.53
  109.7 2.1 copy-start.36
  111.8 12.3 %copy-start.3 = (bf16[448,1024]{1,0:T(8,128)(2,1)}, bf16[448,1024]{1,0:T(8,128)(2,1)S(1)}, u32[]{:S(2)}) copy-start(bf16[448,1024]{1,0:T(8,128)(2,1)S(1)} %gather_fusion) | copy-start | bytes 2752516
  119.3 1.7 copy-start.47
  119.3 27.0 %copy-start.38 = (f32[128,8]{0,1:T(8,128)}, f32[128,8]{0,1:T(8,128)S(1)}, u32[]{:S(2)}) copy-start(f32[128,8]{0,1:T(8,128)S(1)} %get-tuple-element.215) | copy-start | bytes 12292
  120.9 3.5 copy-start.14
  124.4 1.8 copy-start.23
  124.4 3.0 copy-start.6
  126.2 1.9 copy-start.16
  133.6 14.9 %copy-start.9 = (f32[448,1024]{1,0:T(8,128)S(1)}, f32[448,1024]{1,0:T(8,128)}, u32[]{:S(2)}) copy-start(f32[448,1024]{1,0:T(8,128)} %gather_fusion.2) | copy-start | bytes 5505028
  148.4 4.5 copy-start.48
  148.4 4.5 copy-start.2
  152.9 4.0 copy-start.24
  152.9 4.0 copy-start.26
  153.0 2.5 copy-start.15
  162.4 37.9 %copy-start.8 = (f32[128,1024]{1,0:T(8,128)S(1)}, f32[128,1024]{1,0:T(8,128)}, u32[]{:S(2)}) copy-start(f32[128,1024]{1,0:T(8,128)} %copy-done.7) | copy-start | bytes 1572868
  162.4 37.9 %copy-start.37 = (bf16[1024,16]{0,1:T(8,128)(2,1)S(1)}, bf16[1024,16]{0,1:T(8,128)(2,1)}, u32[]{:S(2)}) copy-start(bf16[1024,16]{0,1:T(8,128)(2,1)} %param.22) | copy-start | bytes 98308
  162.4 37.9 %copy-start.40 = (f32[1024]{0:T(1024)S(1)}, f32[1024]{0:T(1024)}, u32[]{:S(2)}) copy-start(f32[1024]{0:T(1024)} %param.21) | copy-start | bytes 12292
  162.4 37.9 %copy-start.54 = (f32[128]{0:T(128)S(1)}, f32[128]{0:T(128)}, u32[]{:S(2)}) copy-start(f32[128]{0:T(128)} %copy-done.53) | copy-start | bytes 1540
  166.7 72.2 %copy-start.11 = (bf16[1024,128]{0,1:T(8,128)(2,1)S(1)}, bf16[1024,128]{0,1:T(8,128)(2,1)}, u32[]{:S(2)}) copy-start(bf16[1024,128]{0,1:T(8,128)(2,1)} %copy-done.10) | copy-start | bytes 786436
  166.7 72.2 %copy-start.13 = (bf16[1024,128]{0,1:T(8,128)(2,1)S(1)}, bf16[1024,128]{0,1:T(8,128)(2,1)}, u32[]{:S(2)}) copy-start(bf16[1024,128]{0,1:T(8,128)(2,1)} %copy-done.12) | copy-start | bytes 786436
  166.7 72.2 %copy-start.52 = (f32[2,2,128]{2,1,0:T(2,128)S(1)}, f32[2,2,128]{2,1,0:T(2,128)}, u32[]{:S(2)}) copy-start(f32[2,2,128]{2,1,0:T(2,128)} %copy-done.51) | copy-start | bytes 6148
  166.8 67.9 %all-reduce.10.cloned.1.call-start = ((), (), s32[]{:S(2)}) async-start(), calls=%async_computation.11 | async-start | bytes 524288 | tf_op jit(solution)/shard_map/psum | solution.py:195
  167.5 139.8 %reduce-scatter.11.cloned.1.call-start = ((), (), s32[]{:S(2)}) async-start(), calls=%async_computation.13 | async-start | bytes 589824 | tf_op jit(solution)/shard_map/reduce_scatter | solution.py:282
  238.9 3.0 copy-start.29
  238.9 3.0 copy-start.31
  239.0 3.5 copy-start.18
  239.0 1.8 copy-start.19
  239.0 1.8 copy-start.21
  241.8 130.6 %copy-start.32 = (bf16[1024,128]{1,0:T(8,128)(2,1)S(1)}, bf16[1024,128]{1,0:T(8,128)(2,1)}, u32[]{:S(2)}) copy-start(bf16[1024,128]{1,0:T(8,128)(2,1)} %param.19) | copy-start | bytes 786436
  241.9 130.6 %reduce-scatter.13.cloned.1.call-start = ((), (), s32[]{:S(2)}) async-start(), calls=%async_computation.14 | async-start | bytes 589824 | tf_op jit(solution)/shard_map/reduce_scatter | solution.py:283
  242.0 134.8 %copy-start.34 = (f32[1024]{0:T(1024)S(1)}, f32[1024]{0:T(1024)}, u32[]{:S(2)}) copy-start(f32[1024]{0:T(1024)} %param.16) | copy-start | bytes 12292
  242.0 134.8 %copy-start.45 = (f32[128]{0:T(128)S(1)}, f32[128]{0:T(128)}, u32[]{:S(2)}) copy-start(f32[128]{0:T(128)} %copy-done.44) | copy-start | bytes 1540
  242.5 165.1 %all-reduce.14.cloned.1.call-start = ((), (), s32[]{:S(2)}) async-start(), calls=%async_computation.15 | async-start | bytes 1048576 | tf_op jit(solution)/shard_map/psum | solution.py:304
  372.5 4.4 copy-start.33
  374.4 6.2 copy-start.17
  374.4 6.2 copy-start.49
  374.5 90.8 %reduce-scatter.23.cloned.1.call-start = ((), (), s32[]{:S(2)}) async-start(), calls=%async_computation.20 | async-start | bytes 73728 | tf_op jit(solution)/shard_map/reduce_scatter | solution.py:325
  375.4 157.2 %reduce-scatter.21.cloned.1.call-start = ((), (), s32[]{:S(2)}) async-start(), calls=%async_computation.19 | async-start | bytes 1179648 | tf_op jit(solution)/shard_map/reduce_scatter | solution.py:323
  376.8 220.7 %reduce-scatter.19.cloned.1.call-start = ((), (), s32[]{:S(2)}) async-start(), calls=%async_computation.18 | async-start | bytes 589824 | tf_op jit(solution)/shard_map/reduce_scatter | solution.py:322
  378.0 284.5 %reduce-scatter.17.cloned.1.call-start = ((), (), s32[]{:S(2)}) async-start(), calls=%async_computation.17 | async-start | bytes 589824 | tf_op jit(solution)/shard_map/reduce_scatter | solution.py:321
  379.2 349.7 %reduce-scatter.15.cloned.1.call-start = ((), (), s32[]{:S(2)}) async-start(), calls=%async_computation.16 | async-start | bytes 1179648 | tf_op jit(solution)/shard_map/reduce_scatter | solution.py:320
  380.6 501.3 %reduce-scatter.29.cloned.1.call-start = ((), (), s32[]{:S(2)}) async-start(), calls=%async_computation.23 | async-start | bytes 9437184 | tf_op jit(solution)/shard_map/reduce_scatter | solution.py:328
  386.7 1.3 copy-start.27
  386.7 1.3 copy-start.42
  386.8 647.8 %reduce-scatter.27.cloned.1.call-start = ((), (), s32[]{:S(2)}) async-start(), calls=%async_computation.22 | async-start | bytes 9437184 | tf_op jit(solution)/shard_map/reduce_scatter | solution.py:327
  392.7 794.9 %reduce-scatter.25.cloned.1.call-start = ((), (), s32[]{:S(2)}) async-start(), calls=%async_computation.21 | async-start | bytes 9437184 | tf_op jit(solution)/shard_map/reduce_scatter | solution.py:326
  398.2 10.5 copy-start.46
  (6 other events, 5.4 us)
Sparse Core Ops, SparseCore 0:
  74.9 32.6 all-reduce.7
  166.9 33.3 all-reduce.11
  202.6 31.9 all-reduce.9
  242.0 65.2 reduce-scatter.10
  311.0 61.3 reduce-scatter.12
  375.3 32.1 all-reduce.13
  411.5 53.6 reduce-scatter.22
  469.6 62.9 reduce-scatter.20
  536.5 60.8 reduce-scatter.18
  601.6 60.8 reduce-scatter.16
  666.4 62.4 reduce-scatter.14
  733.4 148.4 reduce-scatter.28
  886.1 148.4 reduce-scatter.26
  1039.1 148.4 reduce-scatter.24
where the time goes:
time: 1200 us; the launch traced here: 1190 us
  waiting for transfers between devices  975 us (81%)
  blocking collectives  86.6 us (7%)
  matrix products  48.7 us (4%)
  local copies, waits for them, and re-layouts  44 us (4%)
  other arithmetic  23.5 us (2%)
  between operations  15.5 us (1%)
    reduce_scatter x1, waiting for transfers between devices, body(): lax.psum_scatter(down_part, 'ctx', scatter_dimension=2, tiled=True)  153 us
    reduce_scatter x1, waiting for transfers between devices, body(): lax.psum_scatter(gate_part, 'ctx', scatter_dimension=1, tiled=True)  153 us
    reduce_scatter x1, waiting for transfers between devices, body(): lax.psum_scatter(up_part, 'ctx', scatter_dimension=1, tiled=True)  153 us
    reduce_scatter x1, waiting for transfers between devices, body(): lax.psum_scatter(o_part, 'ctx', scatter_dimension=1, tiled=True)  67.3 us
    reduce_scatter x1, waiting for transfers between devices, body(): lax.psum_scatter(q_part, 'ctx', scatter_dimension=0, tiled=True)  66.5 us
    reduce_scatter x1, waiting for transfers between devices, body(): lax.psum_scatter(k_part, 'ctx', scatter_dimension=0, tiled=True)  65 us
    reduce_scatter x1, waiting for transfers between devices, body(): lax.psum_scatter(v_part, 'ctx', scatter_dimension=0, tiled=True)  64.9 us
    reduce_scatter x1, waiting for transfers between devices, body(): lax.psum_scatter(d_key_term, 'ctx', scatter_dimension=0, tiled=True)  64.4 us
  transfers between devices with their start and end apart: 14, of which 14 were waited for; matrix products, arithmetic and copies ran while one was open for 4% of the time, Pallas kernels for 0%

commit v1 on v0

--- a/solution.py
+++ b/solution.py
@@ -152,7 +152,12 @@
     new_top = jnp.maximum(running_top, jnp.max(scores, axis=-1))
     new_total = jnp.sum(jnp.exp(scores - new_top[..., None]), axis=-1)
     log_total = new_top + jnp.log(new_total)
-    key_piece = lax.all_gather(key_rot, "ctx", axis=0, tiled=True)
+    ring = [key_rot]
+    for hop in range(7):
+        ring.append(lax.ppermute(ring[-1], "ctx", [(dev, (dev + 1) % 8) for dev in range(8)]))
+    key_piece = jnp.roll(
+        jnp.concatenate(ring[::-1], axis=0), (lax.axis_index("ctx") + 1) * ring[0].shape[0], axis=0
+    )
     value_piece = lax.all_gather(value_proj, "ctx", axis=0, tiled=True)
     scores = masked_scores(key_piece, jnp.int32(0))
     probs = jnp.exp(scores - log_total[..., None]).astype(jnp.bfloat16)

time: 1200 us -> 1230 us (1.025)
  waiting for transfers between devices: 975 us -> 1010 us
    ppermute x0 -> x7, waiting for transfers between devices: none -> 32.3 us  [body(): lax.ppermute(ring[-1], 'ctx', [(dev, (dev + 1) % 8) for dev in range(8)])]
  transfers between devices with their start and end apart: 14 -> 21, of which waited for: 14 -> 19; matrix products, arithmetic and copies ran while one was open for 4% -> 4% of each run, Pallas kernels for 0% -> 0%
where the time goes in v1:
time: 1230 us
  waiting for transfers between devices  1010 us (82%)
  blocking collectives  85.7 us (7%)
  matrix products  46.4 us (4%)
  local copies, waits for them, and re-layouts  45 us (4%)
  other arithmetic  25.5 us (2%)
  between operations  15.5 us (1%)
    reduce_scatter x1, waiting for transfers between devices, body(): lax.psum_scatter(gate_part, 'ctx', scatter_dimension=1, tiled=True)  153 us
    reduce_scatter x1, waiting for transfers between devices, body(): lax.psum_scatter(down_part, 'ctx', scatter_dimension=2, tiled=True)  153 us
    reduce_scatter x1, waiting for transfers between devices, body(): lax.psum_scatter(up_part, 'ctx', scatter_dimension=1, tiled=True)  153 us
    reduce_scatter x1, waiting for transfers between devices, body(): lax.psum_scatter(o_part, 'ctx', scatter_dimension=1, tiled=True)  67.3 us
    reduce_scatter x1, waiting for transfers between devices, body(): lax.psum_scatter(q_part, 'ctx', scatter_dimension=0, tiled=True)  66.5 us
    reduce_scatter x1, waiting for transfers between devices, body(): lax.psum_scatter(k_part, 'ctx', scatter_dimension=0, tiled=True)  65.1 us
    reduce_scatter x1, waiting for transfers between devices, body(): lax.psum_scatter(v_part, 'ctx', scatter_dimension=0, tiled=True)  64.9 us
    reduce_scatter x1, waiting for transfers between devices, body(): lax.psum_scatter(d_key_term, 'ctx', scatter_dimension=0, tiled=True)  63.9 us
  transfers between devices with their start and end apart: 21, of which 19 were waited for; matrix products, arithmetic and copies ran while one was open for 4% of the time, Pallas kernels for 0%

profile of v1, /device:TPU:0, one launch (start us, length us, event | category | flops | bytes accessed | tf_op | source)
XLA Modules:
  0.0 1232.6 jit_solution(16448266215680698728)
XLA Ops:
  7.3 1.2 fusion.38
  8.5 1.4 fusion.82
  10.1 3.0 collective-permute-start
  13.1 26.9 %all_gather.8 = bf16[1024,128]{0,1:T(8,128)(2,1)S(1)} all-gather(bf16[128,128]{0,1:T(8,128)(2,1)S(1)} %fusion.57), channel_id=1, replica_groups=mesh['ctx'=8,'shard'=4] {'ctx'}, dimensions={0}, use_global_device_ids=true | all-gather | bytes 294912 | tf_op jit(solution)/shard_map/all_gather | solution.py:151
  40.0 1.4 convolution_convert_fusion.1
  43.3 6.5 collective-permute-done.1
  50.0 6.3 collective-permute-done.2
  56.4 6.5 collective-permute-done.3
  63.0 6.5 collective-permute-done.4
  69.7 6.5 collective-permute-done.5
  76.2 30.7 %all_gather.9 = bf16[1024,128]{1,0:T(8,128)(2,1)S(1)} all-gather(bf16[128,128]{1,0:T(8,128)(2,1)S(1)} %convolution_convert_fusion.1), channel_id=1, replica_groups=mesh['ctx'=8,'shard'=4] {'ctx'}, dimensions={0}, use_global_device_ids=true | all-gather | bytes 294912 | tf_op jit(solution)/shard_map/all_gather | solution.py:161
  108.3 1.0 fusion.87
  109.8 7.1 gather_fusion.5
  117.2 2.6 gather_fusion.2
  120.4 23.7 %all-reduce.8.cloned.1.call-done = f32[128,1024]{1,0:T(8,128)} async-done(((f32[128,1024]{1,0:T(8,128)}), f32[128,1024]{1,0:T(8,128)}) %all-reduce.8.cloned.1.call-update) | async-done | bytes 524304 | tf_op jit(solution)/shard_map/psum | solution.py:174
  144.1 1.2 multiply_reduce_fusion.2
  146.2 2.1 gather_fusion
  148.5 7.0 gather_fusion.4
  157.5 3.1 fusion.32
  160.9 1.8 multiply_convert_fusion.3
  162.8 1.2 copy-done.6
  164.7 5.4 gather_fusion.1
  170.1 4.6 fusion.15
  174.8 1.5 copy.150
  176.3 1.3 broadcast_select_fusion.5
  177.5 6.4 psum.38
  187.5 4.5 multiply_convert_fusion.1
  192.0 1.4 fusion.90
  193.4 1.1 copy-done.13
  194.5 1.5 convolution_add_fusion
  196.0 5.4 gather_fusion.3
  201.4 4.4 fusion.14
  206.8 32.4 %all-reduce.12.cloned.1.call-done = f32[128,1024]{1,0:T(8,128)} async-done(((f32[128,1024]{1,0:T(8,128)}), f32[128,1024]{1,0:T(8,128)}) %all-reduce.12.cloned.1.call-update) | async-done | bytes 524304 | tf_op jit(solution)/shard_map/psum | solution.py:222
  239.2 2.3 multiply_reduce_fusion
  241.6 32.0 %all-reduce.10.cloned.1.call-done = bf16[128,1024]{1,0:T(8,128)(2,1)} async-done(((bf16[128,1024]{1,0:T(8,128)(2,1)}), bf16[128,1024]{1,0:T(8,128)(2,1)}) %all-reduce.10.cloned.1.call-update) | async-done | bytes 262160 | tf_op jit(solution)/shard_map/psum | solution.py:200
  273.6 2.2 subtract_add_fusion
  276.2 0.8 broadcast_in_dim.200.clone
  277.1 0.8 broadcast_in_dim.200
  277.9 2.6 while.15
  281.9 63.9 %reduce-scatter.11.cloned.1.call-done = f32[128,128]{0,1:T(8,128)} async-done(((f32[1024,128]{0,1:T(8,128)}), f32[128,128]{0,1:T(8,128)}) %reduce-scatter.11.cloned.1.call-update) | async-done | bytes 65552 | tf_op jit(solution)/shard_map/reduce_scatter | solution.py:287
  346.6 0.9 fusion.59
  347.8 63.2 %reduce-scatter.13.cloned.1.call-done = f32[128,128]{0,1:T(8,128)} async-done(((f32[1024,128]{0,1:T(8,128)}), f32[128,128]{0,1:T(8,128)}) %reduce-scatter.13.cloned.1.call-update) | async-done | bytes 65552 | tf_op jit(solution)/shard_map/reduce_scatter | solution.py:288
  411.0 1.9 convolution_add_fusion.1
  413.9 1.3 fusion.53
  415.3 1.1 fusion.60
  416.5 1.1 fusion.75
  417.7 1.3 fusion.77
  419.1 6.0 fusion.46
  425.3 1.1 copy-done.4
  426.5 4.6 fusion.29
  431.1 0.9 copy-done.22
  432.1 4.6 fusion.30
  438.6 7.5 all-reduce.14.cloned.1.call-done
  446.1 1.2 fusion.41
  447.3 21.6 %all-reduce.2 = (f32[1024]{0:T(1024)S(1)}, f32[1024]{0:T(1024)S(1)}) all-reduce(f32[1024]{0:T(1024)S(1)} %get-tuple-element.184, f32[1024]{0:T(1024)S(1)} %get-tuple-element.182), channel_id=4, replica_groups=mesh['ctx'=8,'shard'=4] {'ctx'}, use_global_device_ids=true, to_apply=%region_30.31.clone | all-reduce | flops 2048 | bytes 16384
  470.1 2.0 fusion.37
  472.2 31.6 %reduce-scatter.23.cloned.1.call-done = f32[128,16]{0,1:T(8,128)} async-done(((f32[1024,16]{0,1:T(8,128)}), f32[128,16]{0,1:T(8,128)}) %reduce-scatter.23.cloned.1.call-update) | async-done | bytes 8208 | tf_op jit(solution)/shard_map/reduce_scatter | solution.py:330
  503.8 67.3 %reduce-scatter.21.cloned.1.call-done = f32[256,128]{1,0:T(8,128)} async-done(((f32[256,1024]{1,0:T(8,128)}), f32[256,128]{1,0:T(8,128)}) %reduce-scatter.21.cloned.1.call-update) | async-done | bytes 131088 | tf_op jit(solution)/shard_map/reduce_scatter | solution.py:328
  571.1 64.9 %reduce-scatter.19.cloned.1.call-done = f32[128,128]{1,0:T(8,128)} async-done(((f32[1024,128]{1,0:T(8,128)}), f32[128,128]{1,0:T(8,128)}) %reduce-scatter.19.cloned.1.call-update) | async-done | bytes 65552 | tf_op jit(solution)/shard_map/reduce_scatter | solution.py:327
  636.0 65.1 %reduce-scatter.17.cloned.1.call-done = f32[128,128]{1,0:T(8,128)} async-done(((f32[1024,128]{1,0:T(8,128)}), f32[128,128]{1,0:T(8,128)}) %reduce-scatter.17.cloned.1.call-update) | async-done | bytes 65552 | tf_op jit(solution)/shard_map/reduce_scatter | solution.py:326
  701.1 66.5 %reduce-scatter.15.cloned.1.call-done = f32[128,256]{1,0:T(8,128)} async-done(((f32[1024,256]{1,0:T(8,128)}), f32[128,256]{1,0:T(8,128)}) %reduce-scatter.15.cloned.1.call-update) | async-done | bytes 131088 | tf_op jit(solution)/shard_map/reduce_scatter | solution.py:325
  767.6 152.9 %reduce-scatter.29.cloned.1.call-done = f32[4,512,128]{2,1,0:T(8,128)} async-done(((f32[4,512,1024]{2,1,0:T(8,128)}), f32[4,512,128]{2,1,0:T(8,128)}) %reduce-scatter.29.cloned.1.call-update) | async-done | bytes 1048592 | tf_op jit(solution)/shard_map/reduce_scatter | solution.py:333
  920.5 152.6 %reduce-scatter.27.cloned.1.call-done = f32[4,128,512]{2,1,0:T(8,128)} async-done(((f32[4,1024,512]{2,1,0:T(8,128)}), f32[4,128,512]{2,1,0:T(8,128)}) %reduce-scatter.27.cloned.1.call-update) | async-done | bytes 1048592 | tf_op jit(solution)/shard_map/reduce_scatter | solution.py:332
  1073.1 152.9 %reduce-scatter.25.cloned.1.call-done = f32[4,128,512]{2,1,0:T(8,128)} async-done(((f32[4,1024,512]{2,1,0:T(8,128)}), f32[4,128,512]{2,1,0:T(8,128)}) %reduce-scatter.25.cloned.1.call-update) | async-done | bytes 1048592 | tf_op jit(solution)/shard_map/reduce_scatter | solution.py:331
  (234 shorter events, 22.9 us)
Async XLA Ops:
  7.2 101.1 %copy-start = (bf16[256,1024]{1,0:T(8,128)(2,1)S(1)}, bf16[256,1024]{1,0:T(8,128)(2,1)}, u32[]{:S(2)}) copy-start(bf16[256,1024]{1,0:T(8,128)(2,1)} %param.20) | copy-start | bytes 1572868
  7.2 34.3 %copy-start.5 = (bf16[128,1024]{1,0:T(8,128)(2,1)S(1)}, bf16[128,1024]{1,0:T(8,128)(2,1)}, u32[]{:S(2)}) copy-start(bf16[128,1024]{1,0:T(8,128)(2,1)} %param.15) | copy-start | bytes 786436
  7.2 34.3 %copy-start.30 = (f32[1024]{0:T(1024)S(1)}, f32[1024]{0:T(1024)}, u32[]{:S(2)}) copy-start(f32[1024]{0:T(1024)} %param.16) | copy-start | bytes 12292
  7.2 34.3 %copy-start.18 = (bf16[1024,256]{1,0:T(8,128)(2,1)S(1)}, bf16[1024,256]{1,0:T(8,128)(2,1)}, u32[]{:S(2)}) copy-start(bf16[1024,256]{1,0:T(8,128)(2,1)} %param.17) | copy-start | bytes 1572868
  7.2 136.9 %all-reduce.8.cloned.1.call-start = ((), (), s32[]{:S(2)}) async-start(), calls=%async_computation.10 | async-start | bytes 1048576 | tf_op jit(solution)/shard_map/psum | solution.py:174
  8.5 33.5 %copy-start.40 = (f32[128]{0:T(128)}, f32[128]{0:T(128)S(1)}, u32[]{:S(2)}) copy-start(f32[128]{0:T(128)S(1)} %add_rsqrt_fusion.1) | copy-start | bytes 1540
  10.1 33.0 %collective-permute-start = (bf16[128,128]{0,1:T(8,128)(2,1)S(1)}, bf16[128,128]{0,1:T(8,128)(2,1)S(1)}, u32[]{:S(2)}, u32[]{:S(2)}) collective-permute-start(bf16[128,128]{0,1:T(8,128)(2,1)S(1)} %fusion.57), channel_id=1, source_target_pairs={{0,4},{4,8},{8,12},{12,16},{16,20},{20,24},{24,28},{28,0},{1,5},{5... | collective-permute-start | bytes 98312 | tf_op jit(solution)/shard_map/ppermute | solution.py:157
  40.0 2.5 copy-start.10
  43.1 6.7 collective-permute-start.1
  43.3 65.0 %copy-start.46 = (f32[2,2,128]{2,1,0:T(2,128)}, f32[2,2,128]{2,1,0:T(2,128)S(1)}, u32[]{:S(2)}) copy-start(f32[2,2,128]{2,1,0:T(2,128)S(1)} %log_add_fusion) | copy-start | bytes 6148
  49.7 6.6 collective-permute-start.2
  56.3 6.6 collective-permute-start.3
  63.0 6.6 collective-permute-start.4
  63.0 56.8 %copy-start.43 = (pred[4,128]{1,0:T(4,128)(4,1)}, pred[4,128]{1,0:T(4,128)(4,1)S(1)}, u32[]{:S(2)}) copy-start(pred[4,128]{1,0:T(4,128)(4,1)S(1)} %fusion.66) | copy-start | bytes 1540
  63.0 56.7 %copy-start.39 = (s32[4,128]{1,0:T(4,128)}, s32[4,128]{1,0:T(4,128)S(1)}, u32[]{:S(2)}) copy-start(s32[4,128]{1,0:T(4,128)S(1)} %copy.146) | copy-start | bytes 6148
  69.6 6.6 collective-permute-start.5
  76.2 30.9 %collective-permute-start.6 = (bf16[128,128]{0,1:T(8,128)(2,1)S(1)}, bf16[128,128]{0,1:T(8,128)(2,1)S(1)}, u32[]{:S(2)}, u32[]{:S(2)}) collective-permute-start(bf16[128,128]{0,1:T(8,128)(2,1)S(1)} %collective-permute-done.5), channel_id=1, source_target_pairs={{0,4},{4,8},{8,12},{12,16},{16,20},{20,24},{24,28},{28,0},{1,5},{5... | collective-permute-start | bytes 98312 | tf_op jit(solution)/shard_map/ppermute | solution.py:157
  107.1 1.2 copy-start.14
  108.3 1.4 copy-start.25
  109.4 129.8 %all-reduce.12.cloned.1.call-start = ((), (), s32[]{:S(2)}) async-start(), calls=%async_computation.12 | async-start | bytes 1048576 | tf_op jit(solution)/shard_map/psum | solution.py:222
  109.8 7.3 copy-start.1
  117.1 28.9 %copy-start.35 = (f32[1024]{0:T(1024)S(1)}, f32[1024]{0:T(1024)}, u32[]{:S(2)}) copy-start(f32[1024]{0:T(1024)} %param.21) | copy-start | bytes 12292
  146.2 2.1 copy-start.32
  148.4 12.3 copy-start.3
  155.8 1.7 copy-start.42
  157.5 3.5 copy-start.12
  157.5 3.4 copy-start.37
  160.9 1.8 copy-start.20
  160.9 3.0 copy-start.6
  162.8 1.9 copy-start.16
  170.1 17.3 %copy-start.9 = (f32[448,1024]{1,0:T(8,128)S(1)}, f32[448,1024]{1,0:T(8,128)}, u32[]{:S(2)}) copy-start(f32[448,1024]{1,0:T(8,128)} %gather_fusion.2) | copy-start | bytes 5505028
  187.5 4.5 copy-start.2
  192.0 1.5 copy-start.21
  192.0 1.5 copy-start.23
  192.0 2.5 copy-start.13
  201.4 37.8 %copy-start.8 = (f32[128,1024]{1,0:T(8,128)S(1)}, f32[128,1024]{1,0:T(8,128)}, u32[]{:S(2)}) copy-start(f32[128,1024]{1,0:T(8,128)} %copy-done.7) | copy-start | bytes 1572868
  201.4 37.8 %copy-start.33 = (bf16[1024,16]{0,1:T(8,128)(2,1)S(1)}, bf16[1024,16]{0,1:T(8,128)(2,1)}, u32[]{:S(2)}) copy-start(bf16[1024,16]{0,1:T(8,128)(2,1)} %param.22) | copy-start | bytes 98308
  201.4 37.8 %copy-start.34 = (f32[128,16]{0,1:T(8,128)S(1)}, f32[128,16]{0,1:T(8,128)}, u32[]{:S(2)}) copy-start(f32[128,16]{0,1:T(8,128)} %get-tuple-element.186) | copy-start | bytes 24580
  201.4 37.8 %copy-start.36 = (f32[1024]{0:T(1024)S(1)}, f32[1024]{0:T(1024)}, u32[]{:S(2)}) copy-start(f32[1024]{0:T(1024)} %param.21) | copy-start | bytes 12292
  201.4 37.8 %copy-start.45 = (f32[128]{0:T(128)S(1)}, f32[128]{0:T(128)}, u32[]{:S(2)}) copy-start(f32[128]{0:T(128)} %copy-done.44) | copy-start | bytes 1540
  205.8 67.8 %all-reduce.10.cloned.1.call-start = ((), (), s32[]{:S(2)}) async-start(), calls=%async_computation.11 | async-start | bytes 524288 | tf_op jit(solution)/shard_map/psum | solution.py:200
  206.5 139.3 %reduce-scatter.11.cloned.1.call-start = ((), (), s32[]{:S(2)}) async-start(), calls=%async_computation.13 | async-start | bytes 589824 | tf_op jit(solution)/shard_map/reduce_scatter | solution.py:287
  241.6 34.6 %copy-start.26 = (bf16[2,2,128,64]{2,3,1,0:T(8,128)(2,1)S(1)}, bf16[2,2,128,64]{2,3,1,0:T(8,128)(2,1)}, u32[]{:S(2)}) copy-start(bf16[2,2,128,64]{2,3,1,0:T(8,128)(2,1)} %copy-done.25) | copy-start | bytes 196612
  273.5 4.4 copy-start.11
  273.5 4.4 copy-start.15
  273.5 4.4 copy-start.47
  280.6 66.9 %copy-start.27 = (bf16[1024,128]{1,0:T(8,128)(2,1)S(1)}, bf16[1024,128]{1,0:T(8,128)(2,1)}, u32[]{:S(2)}) copy-start(bf16[1024,128]{1,0:T(8,128)(2,1)} %param.18) | copy-start | bytes 786436
  280.6 130.4 %reduce-scatter.13.cloned.1.call-start = ((), (), s32[]{:S(2)}) async-start(), calls=%async_computation.14 | async-start | bytes 589824 | tf_op jit(solution)/shard_map/reduce_scatter | solution.py:288
  280.7 130.3 %copy-start.28 = (bf16[1024,128]{1,0:T(8,128)(2,1)S(1)}, bf16[1024,128]{1,0:T(8,128)(2,1)}, u32[]{:S(2)}) copy-start(bf16[1024,128]{1,0:T(8,128)(2,1)} %param.19) | copy-start | bytes 786436
  281.2 164.9 %all-reduce.14.cloned.1.call-start = ((), (), s32[]{:S(2)}) async-start(), calls=%async_computation.15 | async-start | bytes 1048576 | tf_op jit(solution)/shard_map/psum | solution.py:309
  412.9 2.4 copy-start.29
  412.9 2.4 copy-start.41
  412.9 90.9 %reduce-scatter.23.cloned.1.call-start = ((), (), s32[]{:S(2)}) async-start(), calls=%async_computation.20 | async-start | bytes 73728 | tf_op jit(solution)/shard_map/reduce_scatter | solution.py:330
  413.8 157.3 %reduce-scatter.21.cloned.1.call-start = ((), (), s32[]{:S(2)}) async-start(), calls=%async_computation.19 | async-start | bytes 1179648 | tf_op jit(solution)/shard_map/reduce_scatter | solution.py:328
  415.2 220.8 %reduce-scatter.19.cloned.1.call-start = ((), (), s32[]{:S(2)}) async-start(), calls=%async_computation.18 | async-start | bytes 589824 | tf_op jit(solution)/shard_map/reduce_scatter | solution.py:327
  416.4 2.7 copy-start.17
  416.4 284.6 %reduce-scatter.17.cloned.1.call-start = ((), (), s32[]{:S(2)}) async-start(), calls=%async_computation.17 | async-start | bytes 589824 | tf_op jit(solution)/shard_map/reduce_scatter | solution.py:326
  417.7 349.9 %reduce-scatter.15.cloned.1.call-start = ((), (), s32[]{:S(2)}) async-start(), calls=%async_computation.16 | async-start | bytes 1179648 | tf_op jit(solution)/shard_map/reduce_scatter | solution.py:325
  419.1 501.4 %reduce-scatter.29.cloned.1.call-start = ((), (), s32[]{:S(2)}) async-start(), calls=%async_computation.23 | async-start | bytes 9437184 | tf_op jit(solution)/shard_map/reduce_scatter | solution.py:333
  425.2 1.2 copy-start.4
  425.2 1.3 copy-start.24
  425.2 1.3 copy-start.38
  425.2 647.9 %reduce-scatter.27.cloned.1.call-start = ((), (), s32[]{:S(2)}) async-start(), calls=%async_computation.22 | async-start | bytes 9437184 | tf_op jit(solution)/shard_map/reduce_scatter | solution.py:332
  431.1 795.0 %reduce-scatter.25.cloned.1.call-start = ((), (), s32[]{:S(2)}) async-start(), calls=%async_computation.21 | async-start | bytes 9437184 | tf_op jit(solution)/shard_map/reduce_scatter | solution.py:331
  (6 other events, 5.4 us)
Sparse Core Ops, SparseCore 0:
  109.5 34.5 all-reduce.7
  205.9 33.2 all-reduce.11
  241.5 31.9 all-reduce.9
  280.7 65.0 reduce-scatter.10
  349.5 61.4 reduce-scatter.12
  413.9 32.1 all-reduce.13
  450.1 53.6 reduce-scatter.22
  508.2 62.8 reduce-scatter.20
  575.1 60.8 reduce-scatter.18
  640.1 60.9 reduce-scatter.16
  705.1 62.4 reduce-scatter.14
  772.1 148.3 reduce-scatter.28
  924.7 148.3 reduce-scatter.26
  1077.6 148.3 reduce-scatter.24
